TPU v7x, 32 devices: a whole 2x2x4 slice. The times are simulated.
32 devices in a mesh: dp: 8 (over y, x, core), tensor: 4 (over z).
Axes of the slice: x: 2, y: 2, z: 4, core: 2. Of those that a mesh axis runs over, the one named last changes fastest.
Arguments:
- tokens: bfloat16 [16, 1024, 1024], P('dp', 'tensor'), may hold values from -6 to 6
- segments: int32 [16, 1024], P('dp'), may hold values from 0 to 3, as said below
- qkv_weight: bfloat16 [3, 1024, 1024], P(None, None, 'tensor'), may hold values from -0.1875 to 0.1875
- qkv_bias: float32 [3, 1024], P(None, 'tensor'), may hold values from -1.5 to 1.5
- out_weight: bfloat16 [1024, 1024], P('tensor'), may hold values from -0.75 to 0.75
- out_bias: float32 [1024], replicated, may hold values from -1.5 to 1.5
- gain_one: float32 [1024], replicated, may hold values from 0.5 to 1.5
- shift_one: float32 [1024], replicated, may hold values from -1.5 to 1.5
- up_weight: bfloat16 [1024, 4096], P(None, 'tensor'), may hold values from -0.1875 to 0.1875
- up_bias: float32 [4096], P('tensor'), may hold values from -1.5 to 1.5
- down_weight: bfloat16 [4096, 1024], P('tensor'), may hold values from -0.1875 to 0.1875
- down_bias: float32 [1024], replicated, may hold values from -1.5 to 1.5
- gain_two: float32 [1024], replicated, may hold values from 0.5 to 1.5
- shift_two: float32 [1024], replicated, may hold values from -1.5 to 1.5
- proj_weight: bfloat16 [1024, 288], replicated, may hold values from -0.1875 to 0.1875
- out_grad: bfloat16 [16, 1024, 1024], P('dp', 'tensor'), may hold values from -6 to 6
- embed_grad: bfloat16 [16, 1024, 288], P('dp', 'tensor'), may hold values from -6 to 6
Outputs:
- layer_out: bfloat16 [16, 1024, 1024], P('dp', 'tensor')
- embeddings: bfloat16 [16, 1024, 288], P('dp', 'tensor')
- tokens_grad: float32 [16, 1024, 1024], P('dp', 'tensor')
- qkv_weight_grad: float32 [3, 1024, 1024], P(None, None, 'tensor')
- qkv_bias_grad: float32 [3, 1024], P(None, 'tensor')
- out_weight_grad: float32 [1024, 1024], P('tensor')
- out_bias_grad: float32 [1024], replicated
- gain_one_grad: float32 [1024], replicated
- shift_one_grad: float32 [1024], replicated
- up_weight_grad: float32 [1024, 4096], P(None, 'tensor')
- up_bias_grad: float32 [4096], P('tensor')
- down_weight_grad: float32 [4096, 1024], P('tensor')
- down_bias_grad: float32 [1024], replicated
- gain_two_grad: float32 [1024], replicated
- shift_two_grad: float32 [1024], replicated
- proj_weight_grad: float32 [1024, 288], replicated
Inputs may be any that keep to these rules, and one draw needn't show every extreme that they name: `segments`: segment numbers never fall along a sequence; every sequence holds 4 documents, each of at least 200 tokens, and in every sequence some document has exactly 200.
All inputs are finite; a program needn't handle non-finite values.
Results may differ from a plain program's by a relative error of at most 0.018.
Values may be sent and summed in bfloat16 or wider, within the bound.
A program may use at most 192 MiB of HBM per device.

v0:
```python
import math
import jax
import jax.numpy as jnp
from jax import lax
from jax.sharding import PartitionSpec as P

HEAD_DIM = 64
eps = 1e-05


def as_sent(array):

    def short(part):
        return part.astype(jnp.bfloat16) if part.dtype == jnp.float32 else part

    return jax.tree.map(short, array)


def doc_positions(segment_rows):
    length = segment_rows.shape[-1]
    row_index = jnp.broadcast_to(jnp.arange(length, dtype=jnp.int32), segment_rows.shape)
    change = jnp.concatenate(
        [
            jnp.ones(segment_rows.shape[:-1] + (1,), jnp.bool_),
            segment_rows[..., 1:] != segment_rows[..., :-1],
        ],
        axis=-1,
    )
    doc_start = lax.cummax(
        jnp.where(change, row_index, jnp.zeros_like(row_index)), axis=segment_rows.ndim - 1
    )
    return row_index - doc_start


def rotary_tables(positions, head_dim):
    half_dim = head_dim // 2
    exponent = jnp.arange(half_dim, dtype=jnp.float32) * (2.0 / head_dim)
    frequency = jnp.exp(-exponent * math.log(10000.0))
    angles = positions.astype(jnp.float32)[..., None] * frequency
    angles = jnp.concatenate([angles, angles], axis=-1)
    return (jnp.cos(angles), jnp.sin(angles))


def rotate(field, cosine, sine):
    half_dim = field.shape[-1] // 2
    rotated = jnp.concatenate([-field[..., half_dim:], field[..., :half_dim]], axis=-1)
    return field * cosine + rotated * sine


def rotate_back(field, cosine, sine):
    half_dim = field.shape[-1] // 2
    rotated = jnp.concatenate([-field[..., half_dim:], field[..., :half_dim]], axis=-1)
    return field * cosine - rotated * sine


def norm_forward(field, gain, shift):
    row_mean = jnp.mean(field, axis=-1, keepdims=True)
    centred = field - row_mean
    variance = jnp.mean(centred * centred, axis=-1, keepdims=True)
    inv_std = lax.rsqrt(variance + eps)
    scaled = centred * inv_std
    return (scaled * gain + shift, scaled, inv_std)


def norm_backward(upstream, scaled, inv_std, gain):
    grad_scaled = upstream * gain
    grad_input = inv_std * (
        grad_scaled
        - jnp.mean(grad_scaled, axis=-1, keepdims=True)
        - scaled * jnp.mean(grad_scaled * scaled, axis=-1, keepdims=True)
    )
    return (grad_input, jnp.sum(upstream * scaled, axis=(0, 1)), jnp.sum(upstream, axis=(0, 1)))


def device_rows(full_rows, row_count):
    groups, length, model_width = full_rows.shape
    local_rows = length // lax.axis_size("tensor")
    blocks = row_count // (groups * local_rows)
    picked = full_rows
    picked = picked.reshape(groups, blocks, local_rows, model_width).transpose(1, 0, 2, 3)
    return picked.reshape(row_count, model_width)


def masked_scores(queries, keys, seg_row):
    scores = jnp.einsum("hqd,hkd->hqk", queries, keys, preferred_element_type=jnp.float32)
    same_doc = seg_row[:, None] == seg_row[None, :]
    return jnp.where(same_doc[None], scores, -1000000000.0)


def attend(inputs):
    queries, keys, values_low, seg_row = inputs
    scores = masked_scores(queries, keys, seg_row)
    row_peak = jnp.max(scores, axis=-1, keepdims=True)
    shifted = jnp.exp(scores - row_peak)
    row_total = jnp.sum(shifted, axis=-1, keepdims=True)
    probs = (shifted / row_total).astype(jnp.bfloat16)
    mixed_heads = jnp.einsum("hqk,hkd->hqd", probs, values_low, preferred_element_type=jnp.float32)
    return (mixed_heads, row_peak + jnp.log(row_total))


def attend_back(inputs):
    queries, keys, values_low, seg_row, log_total, grad_mixed = inputs
    scores = masked_scores(queries, keys, seg_row)
    probs = jnp.exp(scores - log_total)
    grad_values = jnp.einsum(
        "hqk,hqd->hkd", probs.astype(jnp.bfloat16), grad_mixed, preferred_element_type=jnp.float32
    )
    grad_probs = jnp.einsum(
        "hqd,hkd->hqk", grad_mixed, values_low, preferred_element_type=jnp.float32
    )
    row_inner = jnp.sum(probs * grad_probs, axis=-1, keepdims=True)
    grad_scores = (probs * (grad_probs - row_inner)).astype(jnp.bfloat16)
    grad_queries = jnp.einsum("hqk,hkd->hqd", grad_scores, keys, preferred_element_type=jnp.float32)
    grad_keys = jnp.einsum("hqk,hqd->hkd", grad_scores, queries, preferred_element_type=jnp.float32)
    return (grad_queries, grad_keys, grad_values)


def process(tokens, segments, out_grad, embed_grad, weights):
    (
        qkv_weight,
        qkv_bias,
        out_weight,
        out_bias,
        gain_one,
        shift_one,
        up_weight,
        up_bias,
        down_weight,
        down_bias,
        gain_two,
        shift_two,
        proj_weight,
    ) = weights
    groups, local_rows, model_width = tokens.shape
    length = segments.shape[1]
    heads_here = qkv_weight.shape[2] // HEAD_DIM
    q_scale = HEAD_DIM ** (-0.5)
    cosine, sine = rotary_tables(doc_positions(segments), HEAD_DIM)
    cosine = cosine[:, None]
    sine = sine[:, None]

    def split_heads(field):
        return field.reshape(groups, length, heads_here, HEAD_DIM).transpose(0, 2, 1, 3)

    def join_heads(field):
        return field.transpose(0, 2, 1, 3).reshape(groups, length, heads_here * HEAD_DIM)

    whole_tokens = lax.all_gather(tokens, "tensor", axis=1, tiled=True)
    projected = jnp.einsum(
        "gld,cde->cgle", whole_tokens, qkv_weight, preferred_element_type=jnp.float32
    )
    projected = projected + qkv_bias[:, None, None, :]
    queries = (rotate(split_heads(projected[0]), cosine, sine) * q_scale).astype(jnp.bfloat16)
    keys = rotate(split_heads(projected[1]), cosine, sine).astype(jnp.bfloat16)
    values_low = split_heads(projected[2]).astype(jnp.bfloat16)
    mixed_heads, log_total = lax.map(attend, (queries, keys, values_low, segments))
    mixed = join_heads(mixed_heads).astype(jnp.bfloat16)
    attn_part = lax.psum_scatter(
        jnp.dot(
            device_rows(mixed, lax.axis_size("tensor") * (groups * local_rows)),
            out_weight,
            preferred_element_type=jnp.float32,
        ),
        "tensor",
        scatter_dimension=0,
        tiled=True,
    )
    attn_part = attn_part.reshape(groups, local_rows, model_width)
    first_sum = tokens.astype(jnp.float32) + (attn_part + out_bias)
    normed, scaled_one, inv_one = norm_forward(first_sum, gain_one, shift_one)
    whole_normed = lax.all_gather(normed.astype(jnp.bfloat16), "tensor", axis=1, tiled=True)
    hidden = (
        jnp.einsum("gld,df->glf", whole_normed, up_weight, preferred_element_type=jnp.float32)
        + up_bias
    )
    active = jax.nn.gelu(hidden, approximate=False).astype(jnp.bfloat16)
    ffn_part = lax.psum_scatter(
        jnp.dot(
            device_rows(active, lax.axis_size("tensor") * (groups * local_rows)),
            down_weight,
            preferred_element_type=jnp.float32,
        ),
        "tensor",
        scatter_dimension=0,
        tiled=True,
    )
    second_sum = normed + (ffn_part.reshape(groups, local_rows, model_width) + down_bias)
    result, scaled_two, inv_two = norm_forward(second_sum, gain_two, shift_two)
    result_low = result.astype(jnp.bfloat16)
    embedded = jnp.einsum(
        "gld,dp->glp", result_low, proj_weight, preferred_element_type=jnp.float32
    )
    grad_result = out_grad.astype(jnp.float32) + jnp.einsum(
        "glp,dp->gld", embed_grad, proj_weight, preferred_element_type=jnp.float32
    )
    proj_grad = jnp.einsum(
        "gld,glp->dp", result_low, embed_grad, preferred_element_type=jnp.float32
    )
    grad_second, gain_two_grad, shift_two_grad = norm_backward(
        grad_result, scaled_two, inv_two, gain_two
    )
    second_low = grad_second.astype(jnp.bfloat16)
    down_bias_grad = jnp.sum(second_low.astype(jnp.float32), axis=(0, 1))
    whole_second = lax.all_gather(second_low, "tensor", axis=1, tiled=True)
    down_weight_grad = jnp.einsum(
        "glf,gld->fd", active, whole_second, preferred_element_type=jnp.float32
    )
    grad_active = jnp.einsum(
        "gld,fd->glf", whole_second, down_weight, preferred_element_type=jnp.float32
    )
    gelu_pull = jax.vjp(lambda field: jax.nn.gelu(field, approximate=False), hidden)[1]
    grad_hidden = gelu_pull(grad_active)[0].astype(jnp.bfloat16)
    up_bias_grad = jnp.sum(grad_hidden.astype(jnp.float32), axis=(0, 1))
    up_weight_grad = jnp.einsum(
        "gld,glf->df", whole_normed, grad_hidden, preferred_element_type=jnp.float32
    )
    ffn_back = lax.psum_scatter(
        jnp.einsum(
            "nf,df->nd",
            device_rows(grad_hidden, lax.axis_size("tensor") * (groups * local_rows)),
            up_weight,
            preferred_element_type=jnp.float32,
        ),
        "tensor",
        scatter_dimension=0,
        tiled=True,
    )
    grad_normed = grad_second + ffn_back.reshape(groups, local_rows, model_width)
    grad_first, gain_one_grad, shift_one_grad = norm_backward(
        grad_normed, scaled_one, inv_one, gain_one
    )
    first_low = grad_first.astype(jnp.bfloat16)
    out_bias_grad = jnp.sum(first_low.astype(jnp.float32), axis=(0, 1))
    whole_first = lax.all_gather(first_low, "tensor", axis=1, tiled=True)
    out_weight_grad = jnp.einsum(
        "glh,gld->hd", mixed, whole_first, preferred_element_type=jnp.float32
    )
    grad_mixed = jnp.einsum(
        "gld,hd->glh", whole_first, out_weight, preferred_element_type=jnp.float32
    )
    grad_mixed = split_heads(grad_mixed.astype(jnp.bfloat16))
    grad_queries, grad_keys, grad_values = lax.map(
        attend_back, (queries, keys, values_low, segments, log_total, grad_mixed)
    )
    grad_queries = rotate_back(grad_queries * q_scale, cosine, sine)
    grad_keys = rotate_back(grad_keys, cosine, sine)
    grad_qkv = jnp.stack(
        [join_heads(grad_queries), join_heads(grad_keys), join_heads(grad_values)]
    ).astype(jnp.bfloat16)
    qkv_bias_grad = jnp.sum(grad_qkv.astype(jnp.float32), axis=(1, 2))
    qkv_weight_grad = jnp.einsum(
        "gld,cgle->cde", whole_tokens, grad_qkv, preferred_element_type=jnp.float32
    )
    joined_grad = grad_qkv.transpose(1, 2, 0, 3).reshape(groups, length, 3 * heads_here * HEAD_DIM)
    joined_weight = qkv_weight.transpose(1, 0, 2).reshape(model_width, 3 * heads_here * HEAD_DIM)
    input_back = lax.psum_scatter(
        jnp.einsum(
            "ne,de->nd",
            device_rows(joined_grad, groups * local_rows * lax.axis_size("tensor")),
            joined_weight,
            preferred_element_type=jnp.float32,
        ).astype(jnp.bfloat16),
        "tensor",
        scatter_dimension=0,
        tiled=True,
    ).astype(jnp.float32)
    tokens_grad = grad_first + input_back.reshape(groups, local_rows, model_width)
    sharded_grads = (
        qkv_weight_grad,
        qkv_bias_grad,
        out_weight_grad,
        up_weight_grad,
        up_bias_grad,
        down_weight_grad,
    )
    shared_grads = (
        out_bias_grad,
        gain_one_grad,
        shift_one_grad,
        down_bias_grad,
        gain_two_grad,
        shift_two_grad,
        proj_grad,
    )
    return (result_low, embedded.astype(jnp.bfloat16), tokens_grad, sharded_grads, shared_grads)


def per_device(
    tokens,
    segments,
    qkv_weight,
    qkv_bias,
    out_weight,
    out_bias,
    gain_one,
    shift_one,
    up_weight,
    up_bias,
    down_weight,
    down_bias,
    gain_two,
    shift_two,
    proj_weight,
    out_grad,
    embed_grad,
):
    weights = (
        qkv_weight,
        qkv_bias,
        out_weight,
        out_bias,
        gain_one,
        shift_one,
        up_weight,
        up_bias,
        down_weight,
        down_bias,
        gain_two,
        shift_two,
        proj_weight,
    )

    def one_seq(running, per_seq):
        tok_row, seg_row, dy_row, de_row = per_seq
        results = process(tok_row[None], seg_row[None], dy_row[None], de_row[None], weights)
        running = jax.tree.map(jnp.add, running, (results[3], results[4]))
        return (running, (results[0][0], results[1][0], results[2][0]))

    empty_grads = (
        tuple(
            (
                jnp.zeros(w.shape, jnp.float32)
                for w in (qkv_weight, qkv_bias, out_weight, up_weight, up_bias, down_weight)
            )
        ),
        tuple(
            (
                jnp.zeros(w.shape, jnp.float32)
                for w in (
                    out_bias,
                    gain_one,
                    shift_one,
                    down_bias,
                    gain_two,
                    shift_two,
                    proj_weight,
                )
            )
        ),
    )
    (sharded_grads, shared_grads), (layer_out, embeddings, tokens_grad) = lax.scan(
        one_seq, empty_grads, (tokens, segments, out_grad, embed_grad)
    )
    sharded_grads = jax.tree.map(
        lambda part: part.astype(jnp.float32), lax.psum(as_sent(sharded_grads), "dp")
    )
    shared_grads = lax.psum(shared_grads, ("dp", "tensor"))
    return (
        layer_out,
        embeddings,
        tokens_grad,
        sharded_grads[0],
        sharded_grads[1],
        sharded_grads[2],
        shared_grads[0],
        shared_grads[1],
        shared_grads[2],
        sharded_grads[3],
        sharded_grads[4],
        sharded_grads[5],
        shared_grads[3],
        shared_grads[4],
        shared_grads[5],
        shared_grads[6],
    )


def solution(mesh):
    in_specs = (
        P("dp", "tensor", None),
        P("dp", None),
        P(None, None, "tensor"),
        P(None, "tensor"),
        P("tensor", None),
        P(),
        P(),
        P(),
        P(None, "tensor"),
        P("tensor"),
        P("tensor", None),
        P(),
        P(),
        P(),
        P(),
        P("dp", "tensor", None),
        P("dp", "tensor", None),
    )
    out_specs = (
        P("dp", "tensor", None),
        P("dp", "tensor", None),
        P("dp", "tensor", None),
        P(None, None, "tensor"),
        P(None, "tensor"),
        P("tensor", None),
        P(),
        P(),
        P(),
        P(None, "tensor"),
        P("tensor"),
        P("tensor", None),
        P(),
        P(),
        P(),
        P(),
    )
    return jax.shard_map(
        per_device, mesh=mesh, in_specs=in_specs, out_specs=out_specs, check_vma=False
    )
```

profile of v0, /device:TPU:0, one launch (start us, length us, event | category | flops | bytes accessed | tf_op | source)
XLA Modules:
  0.0 1448.8 jit_solution(7580111649799563815)
XLA Ops:
  10.8 1174.9 %while.6 = (s32[]{:T(128)}, f32[3,1024,256]{1,2,0:T(8,128)}, f32[3,256]{1,0:T(4,128)}, f32[256,1024]{1,0:T(8,128)}, f32[1024,1024]{1,0:T(8,128)}, /*index=5*/f32...) while((s32[]{:T(128)}, f32[3,1024,256]{1,2,0:T(8,128)}, ...), condition=%wide.region_26.27_spmd.clone, body=%wide.region_0.26_spmd.clone.sunk | while | flops 23216961536 | bytes 635246848 | solution.py:351
  17.6 44.3 %all-gather.5.cloned.1.call-done = bf16[1,1024,1024]{2,1,0:T(8,128)(2,1)} async-done(((bf16[1,256,1024]{2,1,0:T(8,128)(2,1)}), bf16[1,1024,1024]{2,1,0:T(8,128)(2,1)}) %all-gather.5.cloned.1.call-update) | async-done | bytes 2097168 | tf_op jit(solution)/shard_map/while/body/eval_jaxpr/all_gather | solution.py:148
  74.1 8.8 fusion.227
  95.1 75.3 %reduce-scatter.5.cloned.1.call-done = f32[256,1024]{1,0:T(8,128)} async-done(((f32[1024,1024]{1,0:T(8,128)}), f32[256,1024]{1,0:T(8,128)}) %reduce-scatter.5.cloned.1.call-update) | async-done | bytes 1048592 | tf_op jit(solution)/shard_map/while/body/eval_jaxpr/reduce_scatter | solution.py:158
  173.2 46.6 %all-gather.7.cloned.1.call-done = bf16[1,1024,1024]{2,1,0:T(8,128)(2,1)} async-done(((bf16[1,256,1024]{2,1,0:T(8,128)(2,1)}), bf16[1,1024,1024]{2,1,0:T(8,128)(2,1)}) %all-gather.7.cloned.1.call-update) | async-done | bytes 2097168 | tf_op jit(solution)/shard_map/while/body/eval_jaxpr/all_gather | solution.py:171
  219.8 14.8 %multiply_convert_fusion.4 = (bf16[1024,1024]{1,0:T(8,128)(2,1)S(1)}, f32[1024,1024]{1,0:T(8,128)}, f32[1024,1024]{1,0:T(8,128)}) fusion(f32[1024]{0:T(1024)S(1)} %copy-done.58, bf16[1024,1024]{1,0:T(8,128)(2,1)} %get-tuple-element.999, bf16[1,1024,1024]{2,1,0:T(8,128)(2,1)} %all-gather.7.cloned.1.call-done), kind=kOutput, calls=%fused_computation.17.clone.1 | convolution fusion | flops 2216689664 | bytes 14684160 | tf_op jit(solution)/shard_map/while/body/eval_jaxpr/gld,df->glf/dot_general | solution.py:173
  240.3 75.6 %reduce-scatter.7.cloned.1.call-done = f32[256,1024]{1,0:T(8,128)} async-done(((f32[1024,1024]{1,0:T(8,128)}), f32[256,1024]{1,0:T(8,128)}) %reduce-scatter.7.cloned.1.call-update) | async-done | bytes 1048592 | tf_op jit(solution)/shard_map/while/body/eval_jaxpr/reduce_scatter | solution.py:177
  322.1 46.0 %all-gather.9.cloned.1.call-done = bf16[1,1024,1024]{2,1,0:T(8,128)(2,1)} async-done(((bf16[1,256,1024]{2,1,0:T(8,128)(2,1)}), bf16[1,1024,1024]{2,1,0:T(8,128)(2,1)}) %all-gather.9.cloned.1.call-update) | async-done | bytes 2097168 | tf_op jit(solution)/shard_map/while/body/eval_jaxpr/all_gather | solution.py:204
  368.0 8.5 convert_reduce_fusion.9
  382.3 75.6 %reduce-scatter.9.cloned.1.call-done = f32[256,1024]{1,0:T(8,128)} async-done(((f32[1024,1024]{1,0:T(8,128)}), f32[256,1024]{1,0:T(8,128)}) %reduce-scatter.9.cloned.1.call-update) | async-done | bytes 1048592 | tf_op jit(solution)/shard_map/while/body/eval_jaxpr/reduce_scatter | solution.py:217
  461.7 46.5 %all-gather.11.cloned.1.call-done = bf16[1,1024,1024]{2,1,0:T(8,128)(2,1)} async-done(((bf16[1,256,1024]{2,1,0:T(8,128)(2,1)}), bf16[1,1024,1024]{2,1,0:T(8,128)(2,1)}) %all-gather.11.cloned.1.call-update) | async-done | bytes 2097168 | tf_op jit(solution)/shard_map/while/body/eval_jaxpr/all_gather | solution.py:234
  510.6 8.7 fusion.236
  519.4 11.8 multiply_reduce_fusion.18
  531.2 12.2 multiply_convert_fusion.5
  576.4 19.7 %reduce-scatter.11.cloned.1.call-done = bf16[256,1024]{1,0:T(8,128)(2,1)} async-done(((bf16[1024,1024]{1,0:T(8,128)(2,1)}), bf16[256,1024]{1,0:T(8,128)(2,1)}) %reduce-scatter.11.cloned.1.call-update) | async-done | bytes 524304 | tf_op jit(solution)/shard_map/while/body/eval_jaxpr/reduce_scatter | solution.py:256
  605.3 40.9 %all-gather.5.cloned.1.call-done = bf16[1,1024,1024]{2,1,0:T(8,128)(2,1)} async-done(((bf16[1,256,1024]{2,1,0:T(8,128)(2,1)}), bf16[1,1024,1024]{2,1,0:T(8,128)(2,1)}) %all-gather.5.cloned.1.call-update) | async-done | bytes 2097168 | tf_op jit(solution)/shard_map/while/body/eval_jaxpr/all_gather | solution.py:148
  658.5 8.8 fusion.227
  679.5 75.1 %reduce-scatter.5.cloned.1.call-done = f32[256,1024]{1,0:T(8,128)} async-done(((f32[1024,1024]{1,0:T(8,128)}), f32[256,1024]{1,0:T(8,128)}) %reduce-scatter.5.cloned.1.call-update) | async-done | bytes 1048592 | tf_op jit(solution)/shard_map/while/body/eval_jaxpr/reduce_scatter | solution.py:158
  757.5 46.6 %all-gather.7.cloned.1.call-done = bf16[1,1024,1024]{2,1,0:T(8,128)(2,1)} async-done(((bf16[1,256,1024]{2,1,0:T(8,128)(2,1)}), bf16[1,1024,1024]{2,1,0:T(8,128)(2,1)}) %all-gather.7.cloned.1.call-update) | async-done | bytes 2097168 | tf_op jit(solution)/shard_map/while/body/eval_jaxpr/all_gather | solution.py:171
  804.1 14.8 %multiply_convert_fusion.4 = (bf16[1024,1024]{1,0:T(8,128)(2,1)S(1)}, f32[1024,1024]{1,0:T(8,128)}, f32[1024,1024]{1,0:T(8,128)}) fusion(f32[1024]{0:T(1024)S(1)} %copy-done.58, bf16[1024,1024]{1,0:T(8,128)(2,1)} %get-tuple-element.999, bf16[1,1024,1024]{2,1,0:T(8,128)(2,1)} %all-gather.7.cloned.1.call-done), kind=kOutput, calls=%fused_computation.17.clone.1 | convolution fusion | flops 2216689664 | bytes 14684160 | tf_op jit(solution)/shard_map/while/body/eval_jaxpr/gld,df->glf/dot_general | solution.py:173
  824.6 75.6 %reduce-scatter.7.cloned.1.call-done = f32[256,1024]{1,0:T(8,128)} async-done(((f32[1024,1024]{1,0:T(8,128)}), f32[256,1024]{1,0:T(8,128)}) %reduce-scatter.7.cloned.1.call-update) | async-done | bytes 1048592 | tf_op jit(solution)/shard_map/while/body/eval_jaxpr/reduce_scatter | solution.py:177
  906.0 46.4 %all-gather.9.cloned.1.call-done = bf16[1,1024,1024]{2,1,0:T(8,128)(2,1)} async-done(((bf16[1,256,1024]{2,1,0:T(8,128)(2,1)}), bf16[1,1024,1024]{2,1,0:T(8,128)(2,1)}) %all-gather.9.cloned.1.call-update) | async-done | bytes 2097168 | tf_op jit(solution)/shard_map/while/body/eval_jaxpr/all_gather | solution.py:204
  966.6 75.6 %reduce-scatter.9.cloned.1.call-done = f32[256,1024]{1,0:T(8,128)} async-done(((f32[1024,1024]{1,0:T(8,128)}), f32[256,1024]{1,0:T(8,128)}) %reduce-scatter.9.cloned.1.call-update) | async-done | bytes 1048592 | tf_op jit(solution)/shard_map/while/body/eval_jaxpr/reduce_scatter | solution.py:217
  1046.0 46.5 %all-gather.11.cloned.1.call-done = bf16[1,1024,1024]{2,1,0:T(8,128)(2,1)} async-done(((bf16[1,256,1024]{2,1,0:T(8,128)(2,1)}), bf16[1,1024,1024]{2,1,0:T(8,128)(2,1)}) %all-gather.11.cloned.1.call-update) | async-done | bytes 2097168 | tf_op jit(solution)/shard_map/while/body/eval_jaxpr/all_gather | solution.py:234
  1095.0 8.7 fusion.236
  1103.7 11.8 multiply_reduce_fusion.18
  1115.5 12.3 multiply_convert_fusion.5
  1163.0 17.5 %reduce-scatter.11.cloned.1.call-done = bf16[256,1024]{1,0:T(8,128)(2,1)} async-done(((bf16[1024,1024]{1,0:T(8,128)(2,1)}), bf16[256,1024]{1,0:T(8,128)(2,1)}) %reduce-scatter.11.cloned.1.call-update) | async-done | bytes 524304 | tf_op jit(solution)/shard_map/while/body/eval_jaxpr/reduce_scatter | solution.py:256
  1197.3 13.8 all-reduce.1
  1212.2 40.5 %all-reduce = (f32[1024]{0:T(1024)}, f32[1024]{0:T(1024)}, f32[1024]{0:T(1024)}, f32[1024]{0:T(1024)}, f32[1024]{0:T(1024)}, /*index=5*/f32[1024]{0:T(1024)}) all-reduce(f32[1024]{0:T(1024)S(1)} %copy-done.49, f32[1024]{0:T(1024)S(1)} %copy-done.46, f32[1024]{0:T(1024)S(1)} %copy-done.43, ...), channel_id=1, replica_groups=mesh['dp'=8,'tensor'=4] {'dp','tensor'}, use_global_device_ids=true, to_apply=%region_30.31 | all-reduce | flops 6144 | bytes 49152 | tf_op jit(solution)/shard_map/psum | solution.py:357
  1252.7 48.6 %all-reduce.8.cloned.1.call-done = (bf16[3,1024,256]{2,1,0:T(8,128)(2,1)}, bf16[256,1024]{1,0:T(8,128)(2,1)}, bf16[1024,1024]{1,0:T(8,128)(2,1)}, bf16[1024,1024]{1,0:T(8,128)(2,1)}) async-done(((bf16[3,1024,256]{2,1,0:T(8,128)(2,1)}, bf16[256,1024]{1,0:T(8,128)(2,1)}, bf16[1024,1024]{1,0:T(8,128)(2,1)}, bf16[1024,1024]{1,0:T(8,128)(2,1)}), (bf16[3,1024,256]{2,1,0:T(8,128)(2,1)}, ...) | async-done | bytes 6291472 | tf_op jit(solution)/shard_map/psum | solution.py:355
  1311.9 127.1 %all-reduce.6.cloned.1.call-done = f32[1024,288]{0,1:T(8,128)} async-done(((f32[1024,288]{0,1:T(8,128)}), f32[1024,288]{0,1:T(8,128)}) %all-reduce.6.cloned.1.call-update) | async-done | bytes 1179664 | tf_op jit(solution)/shard_map/psum | solution.py:357
  (429 shorter events, 223.2 us)
Async XLA Ops:
  10.8 51.1 %all-gather.5.cloned.1.call-start = ((), (), s32[]{:S(2)}) async-start(), calls=%async_computation.6 | async-start | bytes 2621440 | tf_op jit(solution)/shard_map/while/body/eval_jaxpr/all_gather | solution.py:148
  12.7 157.6 %reduce-scatter.5.cloned.1.call-start = ((), (), s32[]{:S(2)}) async-start(), calls=%async_computation.7 | async-start | bytes 5242880 | tf_op jit(solution)/shard_map/while/body/eval_jaxpr/reduce_scatter | solution.py:158
  94.6 75.7 %copy-start.17 = (bf16[2,256,1024]{2,1,0:T(8,128)(2,1)S(1)}, bf16[2,256,1024]{2,1,0:T(8,128)(2,1)}, u32[]{:S(2)}) copy-start(bf16[2,256,1024]{2,1,0:T(8,128)(2,1)} %get-tuple-element.992) | copy-start | bytes 3145732 | tf_op jit(solution)/shard_map/while
  94.6 75.7 %copy-start.50 = (f32[1024]{0:T(1024)S(1)}, f32[1024]{0:T(1024)}, u32[]{:S(2)}) copy-start(f32[1024]{0:T(1024)} %get-tuple-element.996) | copy-start | bytes 12292 | tf_op jit(solution)/shard_map/while
  94.6 77.4 %copy-start.28 = (f32[1024]{0:T(1024)S(1)}, f32[1024]{0:T(1024)}, u32[]{:S(2)}) copy-start(f32[1024]{0:T(1024)} %get-tuple-element.997) | copy-start | bytes 12292 | tf_op jit(solution)/shard_map/while
  94.6 77.4 %copy-start.30 = (f32[1024]{0:T(1024)S(1)}, f32[1024]{0:T(1024)}, u32[]{:S(2)}) copy-start(f32[1024]{0:T(1024)} %get-tuple-element.998) | copy-start | bytes 12292 | tf_op jit(solution)/shard_map/while
  94.6 125.1 %copy-start.58 = (f32[1024]{0:T(1024)S(1)}, f32[1024]{0:T(1024)}, u32[]{:S(2)}) copy-start(f32[1024]{0:T(1024)} %get-tuple-element.1000) | copy-start | bytes 12292 | tf_op jit(solution)/shard_map/while
  94.7 125.1 %all-gather.7.cloned.1.call-start = ((), (), s32[]{:S(2)}) async-start(), calls=%async_computation.8 | async-start | bytes 2621440 | tf_op jit(solution)/shard_map/while/body/eval_jaxpr/all_gather | solution.py:171
  173.1 142.7 %reduce-scatter.7.cloned.1.call-start = ((), (), s32[]{:S(2)}) async-start(), calls=%async_computation.9 | async-start | bytes 5242880 | tf_op jit(solution)/shard_map/while/body/eval_jaxpr/reduce_scatter | solution.py:177
  240.2 75.7 %copy-start.51 = (f32[1024]{0:T(1024)S(1)}, f32[1024]{0:T(1024)}, u32[]{:S(2)}) copy-start(f32[1024]{0:T(1024)} %get-tuple-element.1002) | copy-start | bytes 12292 | tf_op jit(solution)/shard_map/while
  240.2 77.6 %copy-start.31 = (f32[1024]{0:T(1024)S(1)}, f32[1024]{0:T(1024)}, u32[]{:S(2)}) copy-start(f32[1024]{0:T(1024)} %get-tuple-element.1006) | copy-start | bytes 12292 | tf_op jit(solution)/shard_map/while
  240.3 127.8 %all-gather.9.cloned.1.call-start = ((), (), s32[]{:S(2)}) async-start(), calls=%async_computation.10 | async-start | bytes 2621440 | tf_op jit(solution)/shard_map/while/body/eval_jaxpr/all_gather | solution.py:204
  321.4 136.4 %reduce-scatter.9.cloned.1.call-start = ((), (), s32[]{:S(2)}) async-start(), calls=%async_computation.11 | async-start | bytes 5242880 | tf_op jit(solution)/shard_map/while/body/eval_jaxpr/reduce_scatter | solution.py:217
  382.2 125.9 %all-gather.11.cloned.1.call-start = ((), (), s32[]{:S(2)}) async-start(), calls=%async_computation.12 | async-start | bytes 2621440 | tf_op jit(solution)/shard_map/while/body/eval_jaxpr/all_gather | solution.py:234
  461.6 134.5 %reduce-scatter.11.cloned.1.call-start = ((), (), s32[]{:S(2)}) async-start(), calls=%async_computation.13 | async-start | bytes 2621440 | tf_op jit(solution)/shard_map/while/body/eval_jaxpr/reduce_scatter | solution.py:256
  598.5 47.7 %all-gather.5.cloned.1.call-start = ((), (), s32[]{:S(2)}) async-start(), calls=%async_computation.6 | async-start | bytes 2621440 | tf_op jit(solution)/shard_map/while/body/eval_jaxpr/all_gather | solution.py:148
  600.5 154.2 %reduce-scatter.5.cloned.1.call-start = ((), (), s32[]{:S(2)}) async-start(), calls=%async_computation.7 | async-start | bytes 5242880 | tf_op jit(solution)/shard_map/while/body/eval_jaxpr/reduce_scatter | solution.py:158
  679.0 75.7 %copy-start.17 = (bf16[2,256,1024]{2,1,0:T(8,128)(2,1)S(1)}, bf16[2,256,1024]{2,1,0:T(8,128)(2,1)}, u32[]{:S(2)}) copy-start(bf16[2,256,1024]{2,1,0:T(8,128)(2,1)} %get-tuple-element.992) | copy-start | bytes 3145732 | tf_op jit(solution)/shard_map/while
  679.0 75.7 %copy-start.50 = (f32[1024]{0:T(1024)S(1)}, f32[1024]{0:T(1024)}, u32[]{:S(2)}) copy-start(f32[1024]{0:T(1024)} %get-tuple-element.996) | copy-start | bytes 12292 | tf_op jit(solution)/shard_map/while
  679.0 77.4 %copy-start.28 = (f32[1024]{0:T(1024)S(1)}, f32[1024]{0:T(1024)}, u32[]{:S(2)}) copy-start(f32[1024]{0:T(1024)} %get-tuple-element.997) | copy-start | bytes 12292 | tf_op jit(solution)/shard_map/while
  679.0 77.4 %copy-start.30 = (f32[1024]{0:T(1024)S(1)}, f32[1024]{0:T(1024)}, u32[]{:S(2)}) copy-start(f32[1024]{0:T(1024)} %get-tuple-element.998) | copy-start | bytes 12292 | tf_op jit(solution)/shard_map/while
  679.0 125.1 %copy-start.58 = (f32[1024]{0:T(1024)S(1)}, f32[1024]{0:T(1024)}, u32[]{:S(2)}) copy-start(f32[1024]{0:T(1024)} %get-tuple-element.1000) | copy-start | bytes 12292 | tf_op jit(solution)/shard_map/while
  679.0 125.1 %all-gather.7.cloned.1.call-start = ((), (), s32[]{:S(2)}) async-start(), calls=%async_computation.8 | async-start | bytes 2621440 | tf_op jit(solution)/shard_map/while/body/eval_jaxpr/all_gather | solution.py:171
  757.5 142.7 %reduce-scatter.7.cloned.1.call-start = ((), (), s32[]{:S(2)}) async-start(), calls=%async_computation.9 | async-start | bytes 5242880 | tf_op jit(solution)/shard_map/while/body/eval_jaxpr/reduce_scatter | solution.py:177
  824.6 75.7 %copy-start.51 = (f32[1024]{0:T(1024)S(1)}, f32[1024]{0:T(1024)}, u32[]{:S(2)}) copy-start(f32[1024]{0:T(1024)} %get-tuple-element.1002) | copy-start | bytes 12292 | tf_op jit(solution)/shard_map/while
  824.6 77.6 %copy-start.31 = (f32[1024]{0:T(1024)S(1)}, f32[1024]{0:T(1024)}, u32[]{:S(2)}) copy-start(f32[1024]{0:T(1024)} %get-tuple-element.1006) | copy-start | bytes 12292 | tf_op jit(solution)/shard_map/while
  824.6 127.8 %all-gather.9.cloned.1.call-start = ((), (), s32[]{:S(2)}) async-start(), calls=%async_computation.10 | async-start | bytes 2621440 | tf_op jit(solution)/shard_map/while/body/eval_jaxpr/all_gather | solution.py:204
  905.8 136.4 %reduce-scatter.9.cloned.1.call-start = ((), (), s32[]{:S(2)}) async-start(), calls=%async_computation.11 | async-start | bytes 5242880 | tf_op jit(solution)/shard_map/while/body/eval_jaxpr/reduce_scatter | solution.py:217
  966.6 125.9 %all-gather.11.cloned.1.call-start = ((), (), s32[]{:S(2)}) async-start(), calls=%async_computation.12 | async-start | bytes 2621440 | tf_op jit(solution)/shard_map/while/body/eval_jaxpr/all_gather | solution.py:234
  1045.9 134.6 %reduce-scatter.11.cloned.1.call-start = ((), (), s32[]{:S(2)}) async-start(), calls=%async_computation.13 | async-start | bytes 2621440 | tf_op jit(solution)/shard_map/while/body/eval_jaxpr/reduce_scatter | solution.py:256
  1185.7 115.6 %all-reduce.8.cloned.1.call-start = ((), (), s32[]{:S(2)}) async-start(), calls=%async_computation.5 | async-start | bytes 12582912 | tf_op jit(solution)/shard_map/psum | solution.py:355
  1196.6 242.5 %all-reduce.6.cloned.1.call-start = ((), (), s32[]{:S(2)}) async-start(), calls=%async_computation.4 | async-start | bytes 2359296 | tf_op jit(solution)/shard_map/psum | solution.py:357
  (101 other events, 699.8 us)
Sparse Core Ops, SparseCore 0:
  13.2 48.6 all-gather.4
  94.8 75.4 reduce-scatter.4
  173.3 46.4 all-gather.6
  240.4 75.4 reduce-scatter.6
  321.6 46.4 all-gather.8
  382.4 75.4 reduce-scatter.8
  461.7 46.4 all-gather.10
  553.5 42.5 reduce-scatter.10
  600.9 45.2 all-gather.4
  679.1 75.4 reduce-scatter.4
  757.6 46.4 all-gather.6
  824.7 75.4 reduce-scatter.6
  905.9 46.4 all-gather.8
  966.7 75.4 reduce-scatter.8
  1046.0 46.4 all-gather.10
  1137.9 42.5 reduce-scatter.10
Sparse Core Ops, SparseCore 1:
  1196.7 104.6 all-reduce.7
  1308.1 130.9 all-reduce.5
where the time goes:
time: 1450 us
  waiting for transfers between devices  1030 us (71%)
  matrix products  209 us (14%)
  other arithmetic  99.4 us (7%)
  blocking collectives  54.2 us (4%)
  local copies, waits for them, and re-layouts  33.1 us (2%)
  between operations  15.6 us (1%)
    reduce_scatter x2, waiting for transfers between devices, process(): lax.psum_scatter(jnp.einsum('nf,df->nd', device_rows(grad_hidden, lax.axi...  151 us
    reduce_scatter x2, waiting for transfers between devices, process(): lax.psum_scatter(jnp.dot(device_rows(active, lax.axis_size('tensor') * (g...  151 us
    reduce_scatter x2, waiting for transfers between devices, process(): lax.psum_scatter(jnp.dot(device_rows(mixed, lax.axis_size('tensor') * (gr...  150 us
    psum x1, waiting for transfers between devices, per_device(): shared_grads = lax.psum(shared_grads, ('dp', 'tensor'))  127 us
    all_gather x2, waiting for transfers between devices, process(): lax.all_gather(normed.astype(jnp.bfloat16), 'tensor', axis=1, tiled=True)  93.1 us
    all_gather x2, waiting for transfers between devices, process(): whole_first = lax.all_gather(first_low, 'tensor', axis=1, tiled=True)  93 us
    all_gather x2, waiting for transfers between devices, process(): whole_second = lax.all_gather(second_low, 'tensor', axis=1, tiled=True)  92.3 us
    all_gather x2, waiting for transfers between devices, process(): whole_tokens = lax.all_gather(tokens, 'tensor', axis=1, tiled=True)  85.2 us
  transfers between devices with their start and end apart: 18, of which 18 were waited for; matrix products, arithmetic and copies ran while one was open for 4% of the time, Pallas kernels for 0%

commit v1 on v0

--- a/solution.py
+++ b/solution.py
@@ -3,6 +3,7 @@
 import jax.numpy as jnp
 from jax import lax
 from jax.sharding import PartitionSpec as P
+from jax.lax import psum
 
 HEAD_DIM = 64
 eps = 1e-05
@@ -354,7 +355,12 @@
     sharded_grads = jax.tree.map(
         lambda part: part.astype(jnp.float32), lax.psum(as_sent(sharded_grads), "dp")
     )
-    shared_grads = lax.psum(shared_grads, ("dp", "tensor"))
+
+    def pipes_write(mine, dev_axis, comm_axis):
+        field_out = psum(mine, axis_name=dev_axis)
+        return psum(field_out, comm_axis)
+
+    shared_grads = pipes_write(shared_grads, "tensor", "dp")
     return (
         layer_out,
         embeddings,

time: 1450 us -> 1430 us (0.986)
  waiting for transfers between devices: 1030 us -> 1000 us
    psum x1 -> x2, waiting for transfers between devices: 127 us -> 96.7 us  [the longest x1 49.5 us: pipes_write(): return psum(field_out, comm_axis)]
    psum x1 -> x2, blocking collectives: 40.5 us -> 41.2 us  [the longest x1 23.3 us: pipes_write(): return psum(field_out, comm_axis)]
  transfers between devices with their start and end apart: 18 -> 19, of which waited for: 18 -> 19; matrix products, arithmetic and copies ran while one was open for 4% -> 5% of each run, Pallas kernels for 0% -> 0%
where the time goes in v1:
time: 1430 us; the launch traced here: 1420 us
  waiting for transfers between devices  1000 us (70%)
  matrix products  209 us (15%)
  other arithmetic  99.4 us (7%)
  blocking collectives  54.5 us (4%)
  local copies, waits for them, and re-layouts  33.1 us (2%)
  between operations  15.8 us (1%)
    reduce_scatter x2, waiting for transfers between devices, process(): lax.psum_scatter(jnp.einsum('nf,df->nd', device_rows(grad_hidden, lax.axi...  151 us
    reduce_scatter x2, waiting for transfers between devices, process(): lax.psum_scatter(jnp.dot(device_rows(active, lax.axis_size('tensor') * (g...  151 us
    reduce_scatter x2, waiting for transfers between devices, process(): lax.psum_scatter(jnp.dot(device_rows(mixed, lax.axis_size('tensor') * (gr...  150 us
    all_gather x2, waiting for transfers between devices, process(): lax.all_gather(normed.astype(jnp.bfloat16), 'tensor', axis=1, tiled=True)  93.1 us
    all_gather x2, waiting for transfers between devices, process(): whole_first = lax.all_gather(first_low, 'tensor', axis=1, tiled=True)  93 us
    all_gather x2, waiting for transfers between devices, process(): whole_second = lax.all_gather(second_low, 'tensor', axis=1, tiled=True)  92.3 us
    all_gather x2, waiting for transfers between devices, process(): whole_tokens = lax.all_gather(tokens, 'tensor', axis=1, tiled=True)  85.2 us
    psum x1, waiting for transfers between devices, per_device(): lax.psum(as_sent(sharded_grads), 'dp')  52.7 us
  transfers between devices with their start and end apart: 19, of which 19 were waited for; matrix products, arithmetic and copies ran while one was open for 5% of the time, Pallas kernels for 0%

profile of v1, /device:TPU:0, one launch (start us, length us, event | category | flops | bytes accessed | tf_op | source)
XLA Modules:
  0.0 1422.9 jit_solution(14408166346601009069)
XLA Ops:
  10.8 1174.8 %while.6 = (s32[]{:T(128)}, f32[3,1024,256]{1,2,0:T(8,128)}, f32[3,256]{1,0:T(4,128)}, f32[256,1024]{1,0:T(8,128)}, f32[1024,1024]{1,0:T(8,128)}, /*index=5*/f32...) while((s32[]{:T(128)}, f32[3,1024,256]{1,2,0:T(8,128)}, ...), condition=%wide.region_26.27_spmd.clone, body=%wide.region_0.26_spmd.clone.sunk | while | flops 23216961536 | bytes 635246848 | solution.py:352
  17.6 44.3 %all-gather.5.cloned.1.call-done = bf16[1,1024,1024]{2,1,0:T(8,128)(2,1)} async-done(((bf16[1,256,1024]{2,1,0:T(8,128)(2,1)}), bf16[1,1024,1024]{2,1,0:T(8,128)(2,1)}) %all-gather.5.cloned.1.call-update) | async-done | bytes 2097168 | tf_op jit(solution)/shard_map/while/body/eval_jaxpr/all_gather | solution.py:149
  74.1 8.8 fusion.227
  95.0 75.3 %reduce-scatter.5.cloned.1.call-done = f32[256,1024]{1,0:T(8,128)} async-done(((f32[1024,1024]{1,0:T(8,128)}), f32[256,1024]{1,0:T(8,128)}) %reduce-scatter.5.cloned.1.call-update) | async-done | bytes 1048592 | tf_op jit(solution)/shard_map/while/body/eval_jaxpr/reduce_scatter | solution.py:159
  173.1 46.6 %all-gather.7.cloned.1.call-done = bf16[1,1024,1024]{2,1,0:T(8,128)(2,1)} async-done(((bf16[1,256,1024]{2,1,0:T(8,128)(2,1)}), bf16[1,1024,1024]{2,1,0:T(8,128)(2,1)}) %all-gather.7.cloned.1.call-update) | async-done | bytes 2097168 | tf_op jit(solution)/shard_map/while/body/eval_jaxpr/all_gather | solution.py:172
  219.7 14.8 %multiply_convert_fusion.4 = (bf16[1024,1024]{1,0:T(8,128)(2,1)S(1)}, f32[1024,1024]{1,0:T(8,128)}, f32[1024,1024]{1,0:T(8,128)}) fusion(f32[1024]{0:T(1024)S(1)} %copy-done.58, bf16[1024,1024]{1,0:T(8,128)(2,1)} %get-tuple-element.1005, bf16[1,1024,1024]{2,1,0:T(8,128)(2,1)} %all-gather.7.cloned.1.call-done), kind=kOutput, calls=%fused_computation.17.clone.1 | convolution fusion | flops 2216689664 | bytes 14684160 | tf_op jit(solution)/shard_map/while/body/eval_jaxpr/gld,df->glf/dot_general | solution.py:174
  240.3 75.6 %reduce-scatter.7.cloned.1.call-done = f32[256,1024]{1,0:T(8,128)} async-done(((f32[1024,1024]{1,0:T(8,128)}), f32[256,1024]{1,0:T(8,128)}) %reduce-scatter.7.cloned.1.call-update) | async-done | bytes 1048592 | tf_op jit(solution)/shard_map/while/body/eval_jaxpr/reduce_scatter | solution.py:178
  322.0 46.0 %all-gather.9.cloned.1.call-done = bf16[1,1024,1024]{2,1,0:T(8,128)(2,1)} async-done(((bf16[1,256,1024]{2,1,0:T(8,128)(2,1)}), bf16[1,1024,1024]{2,1,0:T(8,128)(2,1)}) %all-gather.9.cloned.1.call-update) | async-done | bytes 2097168 | tf_op jit(solution)/shard_map/while/body/eval_jaxpr/all_gather | solution.py:205
  382.2 75.6 %reduce-scatter.9.cloned.1.call-done = f32[256,1024]{1,0:T(8,128)} async-done(((f32[1024,1024]{1,0:T(8,128)}), f32[256,1024]{1,0:T(8,128)}) %reduce-scatter.9.cloned.1.call-update) | async-done | bytes 1048592 | tf_op jit(solution)/shard_map/while/body/eval_jaxpr/reduce_scatter | solution.py:218
  461.6 46.5 %all-gather.11.cloned.1.call-done = bf16[1,1024,1024]{2,1,0:T(8,128)(2,1)} async-done(((bf16[1,256,1024]{2,1,0:T(8,128)(2,1)}), bf16[1,1024,1024]{2,1,0:T(8,128)(2,1)}) %all-gather.11.cloned.1.call-update) | async-done | bytes 2097168 | tf_op jit(solution)/shard_map/while/body/eval_jaxpr/all_gather | solution.py:235
  510.5 8.7 fusion.236
  519.3 11.8 multiply_reduce_fusion.18
  531.1 12.2 multiply_convert_fusion.5
  576.3 19.7 %reduce-scatter.11.cloned.1.call-done = bf16[256,1024]{1,0:T(8,128)(2,1)} async-done(((bf16[1024,1024]{1,0:T(8,128)(2,1)}), bf16[256,1024]{1,0:T(8,128)(2,1)}) %reduce-scatter.11.cloned.1.call-update) | async-done | bytes 524304 | tf_op jit(solution)/shard_map/while/body/eval_jaxpr/reduce_scatter | solution.py:257
  605.3 40.9 %all-gather.5.cloned.1.call-done = bf16[1,1024,1024]{2,1,0:T(8,128)(2,1)} async-done(((bf16[1,256,1024]{2,1,0:T(8,128)(2,1)}), bf16[1,1024,1024]{2,1,0:T(8,128)(2,1)}) %all-gather.5.cloned.1.call-update) | async-done | bytes 2097168 | tf_op jit(solution)/shard_map/while/body/eval_jaxpr/all_gather | solution.py:149
  658.4 8.8 fusion.227
  679.4 75.1 %reduce-scatter.5.cloned.1.call-done = f32[256,1024]{1,0:T(8,128)} async-done(((f32[1024,1024]{1,0:T(8,128)}), f32[256,1024]{1,0:T(8,128)}) %reduce-scatter.5.cloned.1.call-update) | async-done | bytes 1048592 | tf_op jit(solution)/shard_map/while/body/eval_jaxpr/reduce_scatter | solution.py:159
  757.4 46.5 %all-gather.7.cloned.1.call-done = bf16[1,1024,1024]{2,1,0:T(8,128)(2,1)} async-done(((bf16[1,256,1024]{2,1,0:T(8,128)(2,1)}), bf16[1,1024,1024]{2,1,0:T(8,128)(2,1)}) %all-gather.7.cloned.1.call-update) | async-done | bytes 2097168 | tf_op jit(solution)/shard_map/while/body/eval_jaxpr/all_gather | solution.py:172
  804.0 14.8 %multiply_convert_fusion.4 = (bf16[1024,1024]{1,0:T(8,128)(2,1)S(1)}, f32[1024,1024]{1,0:T(8,128)}, f32[1024,1024]{1,0:T(8,128)}) fusion(f32[1024]{0:T(1024)S(1)} %copy-done.58, bf16[1024,1024]{1,0:T(8,128)(2,1)} %get-tuple-element.1005, bf16[1,1024,1024]{2,1,0:T(8,128)(2,1)} %all-gather.7.cloned.1.call-done), kind=kOutput, calls=%fused_computation.17.clone.1 | convolution fusion | flops 2216689664 | bytes 14684160 | tf_op jit(solution)/shard_map/while/body/eval_jaxpr/gld,df->glf/dot_general | solution.py:174
  824.5 75.6 %reduce-scatter.7.cloned.1.call-done = f32[256,1024]{1,0:T(8,128)} async-done(((f32[1024,1024]{1,0:T(8,128)}), f32[256,1024]{1,0:T(8,128)}) %reduce-scatter.7.cloned.1.call-update) | async-done | bytes 1048592 | tf_op jit(solution)/shard_map/while/body/eval_jaxpr/reduce_scatter | solution.py:178
  905.9 46.4 %all-gather.9.cloned.1.call-done = bf16[1,1024,1024]{2,1,0:T(8,128)(2,1)} async-done(((bf16[1,256,1024]{2,1,0:T(8,128)(2,1)}), bf16[1,1024,1024]{2,1,0:T(8,128)(2,1)}) %all-gather.9.cloned.1.call-update) | async-done | bytes 2097168 | tf_op jit(solution)/shard_map/while/body/eval_jaxpr/all_gather | solution.py:205
  966.5 75.6 %reduce-scatter.9.cloned.1.call-done = f32[256,1024]{1,0:T(8,128)} async-done(((f32[1024,1024]{1,0:T(8,128)}), f32[256,1024]{1,0:T(8,128)}) %reduce-scatter.9.cloned.1.call-update) | async-done | bytes 1048592 | tf_op jit(solution)/shard_map/while/body/eval_jaxpr/reduce_scatter | solution.py:218
  1045.9 46.5 %all-gather.11.cloned.1.call-done = bf16[1,1024,1024]{2,1,0:T(8,128)(2,1)} async-done(((bf16[1,256,1024]{2,1,0:T(8,128)(2,1)}), bf16[1,1024,1024]{2,1,0:T(8,128)(2,1)}) %all-gather.11.cloned.1.call-update) | async-done | bytes 2097168 | tf_op jit(solution)/shard_map/while/body/eval_jaxpr/all_gather | solution.py:235
  1103.5 11.8 multiply_reduce_fusion.18
  1115.4 12.3 multiply_convert_fusion.5
  1162.8 17.5 %reduce-scatter.11.cloned.1.call-done = bf16[256,1024]{1,0:T(8,128)(2,1)} async-done(((bf16[1024,1024]{1,0:T(8,128)(2,1)}), bf16[256,1024]{1,0:T(8,128)(2,1)}) %reduce-scatter.11.cloned.1.call-update) | async-done | bytes 524304 | tf_op jit(solution)/shard_map/while/body/eval_jaxpr/reduce_scatter | solution.py:257
  1197.2 47.1 %all-reduce.8.cloned.1.call-done = f32[1024,288]{0,1:T(8,128)} async-done(((f32[1024,288]{0,1:T(8,128)}), f32[1024,288]{0,1:T(8,128)}) %all-reduce.8.cloned.1.call-update) | async-done | bytes 1179664 | tf_op jit(solution)/shard_map/psum | solution.py:360
  1244.4 13.2 all-reduce.2
  1258.8 17.9 %all-reduce.1 = (f32[1024]{0:T(1024)S(1)}, f32[1024]{0:T(1024)S(1)}, f32[1024]{0:T(1024)S(1)}, f32[1024]{0:T(1024)S(1)}, f32[1024]{0:T(1024)S(1)}, /*index=5*/f32[1024]{0:T(1024)S(1)}) all-reduce(f32[1024]{0:T(1024)S(1)} %copy-done.49, f32[1024]{0:T(1024)S(1)} %copy-done.46, ...), channel_id=1, replica_groups=mesh['dp'=8,'tensor'=4] {'tensor'}, use_global_device_ids=true, to_apply=%region_30.31 | all-reduce | flops 6144 | bytes 49152 | tf_op jit(solution)/shard_map/psum | solution.py:360
  1276.7 23.3 %all-reduce = (f32[1024]{0:T(1024)}, f32[1024]{0:T(1024)}, f32[1024]{0:T(1024)}, f32[1024]{0:T(1024)}, f32[1024]{0:T(1024)}, /*index=5*/f32[1024]{0:T(1024)}) all-reduce(f32[1024]{0:T(1024)S(1)} %get-tuple-element.525, f32[1024]{0:T(1024)S(1)} %get-tuple-element.526, ...), channel_id=1, replica_groups=mesh['dp'=8,'tensor'=4] {'dp'}, use_global_device_ids=true, to_apply=%region_31.32 | all-reduce | flops 6144 | bytes 49152 | tf_op jit(solution)/shard_map/psum | solution.py:361
  1300.1 52.7 %all-reduce.12.cloned.1.call-done = (bf16[3,1024,256]{2,1,0:T(8,128)(2,1)}, bf16[256,1024]{1,0:T(8,128)(2,1)}, bf16[1024,1024]{1,0:T(8,128)(2,1)}, bf16[1024,1024]{1,0:T(8,128)(2,1)}) async-done(((bf16[3,1024,256]{2,1,0:T(8,128)(2,1)}, bf16[256,1024]{1,0:T(8,128)(2,1)}, bf16[1024,1024]{1,0:T(8,128)(2,1)}, bf16[1024,1024]{1,0:T(8,128)(2,1)}), (bf16[3,1024,256]{2,1,0:T(8,128)(2,1)}, ...) | async-done | bytes 6291472 | tf_op jit(solution)/shard_map/psum | solution.py:356
  1363.3 49.5 %all-reduce.10.cloned.1.call-done = f32[1024,288]{0,1:T(8,128)} async-done(((f32[1024,288]{0,1:T(8,128)}), f32[1024,288]{0,1:T(8,128)}) %all-reduce.10.cloned.1.call-update) | async-done | bytes 1179664 | tf_op jit(solution)/shard_map/psum | solution.py:361
  (433 shorter events, 240.3 us)
Async XLA Ops:
  10.8 51.1 %all-gather.5.cloned.1.call-start = ((), (), s32[]{:S(2)}) async-start(), calls=%async_computation.7 | async-start | bytes 2621440 | tf_op jit(solution)/shard_map/while/body/eval_jaxpr/all_gather | solution.py:149
  12.7 157.6 %reduce-scatter.5.cloned.1.call-start = ((), (), s32[]{:S(2)}) async-start(), calls=%async_computation.8 | async-start | bytes 5242880 | tf_op jit(solution)/shard_map/while/body/eval_jaxpr/reduce_scatter | solution.py:159
  94.6 75.7 %copy-start.17 = (bf16[2,256,1024]{2,1,0:T(8,128)(2,1)S(1)}, bf16[2,256,1024]{2,1,0:T(8,128)(2,1)}, u32[]{:S(2)}) copy-start(bf16[2,256,1024]{2,1,0:T(8,128)(2,1)} %get-tuple-element.998) | copy-start | bytes 3145732 | tf_op jit(solution)/shard_map/while
  94.6 75.7 %copy-start.50 = (f32[1024]{0:T(1024)S(1)}, f32[1024]{0:T(1024)}, u32[]{:S(2)}) copy-start(f32[1024]{0:T(1024)} %get-tuple-element.1002) | copy-start | bytes 12292 | tf_op jit(solution)/shard_map/while
  94.6 77.4 %copy-start.28 = (f32[1024]{0:T(1024)S(1)}, f32[1024]{0:T(1024)}, u32[]{:S(2)}) copy-start(f32[1024]{0:T(1024)} %get-tuple-element.1003) | copy-start | bytes 12292 | tf_op jit(solution)/shard_map/while
  94.6 77.4 %copy-start.30 = (f32[1024]{0:T(1024)S(1)}, f32[1024]{0:T(1024)}, u32[]{:S(2)}) copy-start(f32[1024]{0:T(1024)} %get-tuple-element.1004) | copy-start | bytes 12292 | tf_op jit(solution)/shard_map/while
  94.6 125.1 %copy-start.58 = (f32[1024]{0:T(1024)S(1)}, f32[1024]{0:T(1024)}, u32[]{:S(2)}) copy-start(f32[1024]{0:T(1024)} %get-tuple-element.1006) | copy-start | bytes 12292 | tf_op jit(solution)/shard_map/while
  94.6 125.1 %all-gather.7.cloned.1.call-start = ((), (), s32[]{:S(2)}) async-start(), calls=%async_computation.9 | async-start | bytes 2621440 | tf_op jit(solution)/shard_map/while/body/eval_jaxpr/all_gather | solution.py:172
  173.1 142.7 %reduce-scatter.7.cloned.1.call-start = ((), (), s32[]{:S(2)}) async-start(), calls=%async_computation.10 | async-start | bytes 5242880 | tf_op jit(solution)/shard_map/while/body/eval_jaxpr/reduce_scatter | solution.py:178
  240.2 75.7 %copy-start.51 = (f32[1024]{0:T(1024)S(1)}, f32[1024]{0:T(1024)}, u32[]{:S(2)}) copy-start(f32[1024]{0:T(1024)} %get-tuple-element.1008) | copy-start | bytes 12292 | tf_op jit(solution)/shard_map/while
  240.2 77.6 %copy-start.31 = (f32[1024]{0:T(1024)S(1)}, f32[1024]{0:T(1024)}, u32[]{:S(2)}) copy-start(f32[1024]{0:T(1024)} %get-tuple-element.1012) | copy-start | bytes 12292 | tf_op jit(solution)/shard_map/while
  240.2 127.8 %all-gather.9.cloned.1.call-start = ((), (), s32[]{:S(2)}) async-start(), calls=%async_computation.11 | async-start | bytes 2621440 | tf_op jit(solution)/shard_map/while/body/eval_jaxpr/all_gather | solution.py:205
  321.4 136.4 %reduce-scatter.9.cloned.1.call-start = ((), (), s32[]{:S(2)}) async-start(), calls=%async_computation.12 | async-start | bytes 5242880 | tf_op jit(solution)/shard_map/while/body/eval_jaxpr/reduce_scatter | solution.py:218
  382.2 125.9 %all-gather.11.cloned.1.call-start = ((), (), s32[]{:S(2)}) async-start(), calls=%async_computation.13 | async-start | bytes 2621440 | tf_op jit(solution)/shard_map/while/body/eval_jaxpr/all_gather | solution.py:235
  461.5 134.5 %reduce-scatter.11.cloned.1.call-start = ((), (), s32[]{:S(2)}) async-start(), calls=%async_computation.14 | async-start | bytes 2621440 | tf_op jit(solution)/shard_map/while/body/eval_jaxpr/reduce_scatter | solution.py:257
  598.4 47.7 %all-gather.5.cloned.1.call-start = ((), (), s32[]{:S(2)}) async-start(), calls=%async_computation.7 | async-start | bytes 2621440 | tf_op jit(solution)/shard_map/while/body/eval_jaxpr/all_gather | solution.py:149
  600.4 154.1 %reduce-scatter.5.cloned.1.call-start = ((), (), s32[]{:S(2)}) async-start(), calls=%async_computation.8 | async-start | bytes 5242880 | tf_op jit(solution)/shard_map/while/body/eval_jaxpr/reduce_scatter | solution.py:159
  678.8 75.7 %copy-start.17 = (bf16[2,256,1024]{2,1,0:T(8,128)(2,1)S(1)}, bf16[2,256,1024]{2,1,0:T(8,128)(2,1)}, u32[]{:S(2)}) copy-start(bf16[2,256,1024]{2,1,0:T(8,128)(2,1)} %get-tuple-element.998) | copy-start | bytes 3145732 | tf_op jit(solution)/shard_map/while
  678.9 75.7 %copy-start.50 = (f32[1024]{0:T(1024)S(1)}, f32[1024]{0:T(1024)}, u32[]{:S(2)}) copy-start(f32[1024]{0:T(1024)} %get-tuple-element.1002) | copy-start | bytes 12292 | tf_op jit(solution)/shard_map/while
  678.9 77.4 %copy-start.28 = (f32[1024]{0:T(1024)S(1)}, f32[1024]{0:T(1024)}, u32[]{:S(2)}) copy-start(f32[1024]{0:T(1024)} %get-tuple-element.1003) | copy-start | bytes 12292 | tf_op jit(solution)/shard_map/while
  678.9 77.4 %copy-start.30 = (f32[1024]{0:T(1024)S(1)}, f32[1024]{0:T(1024)}, u32[]{:S(2)}) copy-start(f32[1024]{0:T(1024)} %get-tuple-element.1004) | copy-start | bytes 12292 | tf_op jit(solution)/shard_map/while
  678.9 125.1 %copy-start.58 = (f32[1024]{0:T(1024)S(1)}, f32[1024]{0:T(1024)}, u32[]{:S(2)}) copy-start(f32[1024]{0:T(1024)} %get-tuple-element.1006) | copy-start | bytes 12292 | tf_op jit(solution)/shard_map/while
  678.9 125.1 %all-gather.7.cloned.1.call-start = ((), (), s32[]{:S(2)}) async-start(), calls=%async_computation.9 | async-start | bytes 2621440 | tf_op jit(solution)/shard_map/while/body/eval_jaxpr/all_gather | solution.py:172
  757.4 142.7 %reduce-scatter.7.cloned.1.call-start = ((), (), s32[]{:S(2)}) async-start(), calls=%async_computation.10 | async-start | bytes 5242880 | tf_op jit(solution)/shard_map/while/body/eval_jaxpr/reduce_scatter | solution.py:178
  824.4 77.6 %copy-start.31 = (f32[1024]{0:T(1024)S(1)}, f32[1024]{0:T(1024)}, u32[]{:S(2)}) copy-start(f32[1024]{0:T(1024)} %get-tuple-element.1012) | copy-start | bytes 12292 | tf_op jit(solution)/shard_map/while
  824.5 127.8 %all-gather.9.cloned.1.call-start = ((), (), s32[]{:S(2)}) async-start(), calls=%async_computation.11 | async-start | bytes 2621440 | tf_op jit(solution)/shard_map/while/body/eval_jaxpr/all_gather | solution.py:205
  905.6 136.4 %reduce-scatter.9.cloned.1.call-start = ((), (), s32[]{:S(2)}) async-start(), calls=%async_computation.12 | async-start | bytes 5242880 | tf_op jit(solution)/shard_map/while/body/eval_jaxpr/reduce_scatter | solution.py:218
  966.4 125.9 %all-gather.11.cloned.1.call-start = ((), (), s32[]{:S(2)}) async-start(), calls=%async_computation.13 | async-start | bytes 2621440 | tf_op jit(solution)/shard_map/while/body/eval_jaxpr/all_gather | solution.py:235
  1045.8 134.6 %reduce-scatter.11.cloned.1.call-start = ((), (), s32[]{:S(2)}) async-start(), calls=%async_computation.14 | async-start | bytes 2621440 | tf_op jit(solution)/shard_map/while/body/eval_jaxpr/reduce_scatter | solution.py:257
  1185.6 58.7 %all-reduce.8.cloned.1.call-start = ((), (), s32[]{:S(2)}) async-start(), calls=%async_computation.4 | async-start | bytes 2359296 | tf_op jit(solution)/shard_map/psum | solution.py:360
  1186.2 166.6 %all-reduce.12.cloned.1.call-start = ((), (), s32[]{:S(2)}) async-start(), calls=%async_computation.6 | async-start | bytes 12582912 | tf_op jit(solution)/shard_map/psum | solution.py:356
  1197.1 215.7 %all-reduce.10.cloned.1.call-start = ((), (), s32[]{:S(2)}) async-start(), calls=%async_computation.5 | async-start | bytes 2359296 | tf_op jit(solution)/shard_map/psum | solution.py:361
  (102 other events, 1052.8 us)
Sparse Core Ops, SparseCore 0:
  13.2 48.6 all-gather.4
  94.7 75.4 reduce-scatter.4
  173.2 46.4 all-gather.6
  240.3 75.4 reduce-scatter.6
  321.5 46.4 all-gather.8
  382.3 75.4 reduce-scatter.8
  461.6 46.4 all-gather.10
  553.4 42.5 reduce-scatter.10
  600.8 45.2 all-gather.4
  679.0 75.4 reduce-scatter.4
  757.5 46.4 all-gather.6
  824.6 75.4 reduce-scatter.6
  905.8 46.4 all-gather.8
  966.5 75.4 reduce-scatter.8
  1045.9 46.4 all-gather.10
  1137.7 42.5 reduce-scatter.10
Sparse Core Ops, SparseCore 1:
  1189.0 55.2 all-reduce.7
  1249.0 103.7 all-reduce.11
  1356.1 56.7 all-reduce.9
